TPU v7x, 128 devices: a whole 4x4x4 slice. The times are simulated.
128 devices in a mesh: expert: 16 (over x, y), head: 8 (over z, core).
Axes of the slice: x: 4, y: 4, z: 4, core: 2. Of those that a mesh axis runs over, the one named last changes fastest.
Arguments:
- table_cells: bfloat16 [8192, 2, 2048], P(('expert', 'head')), may hold values from -8 to 8
- w_query: bfloat16 [2048, 2048], P(None, 'head')
- w_key: bfloat16 [2048, 2048], P(None, 'head')
- w_value: bfloat16 [2048, 2048], P(None, 'head'), may hold values from -0.125 to 0.125
- w_out: bfloat16 [2048, 2048], P('head'), may hold values from -0.125 to 0.125
- norm_gain: bfloat16 [2048], replicated, may hold values from 0.099609375 to 1.8984375
- w_gate: bfloat16 [128, 704, 2048], P(('expert', 'head')), may hold values from -0.125 to 0.125
- w_up: bfloat16 [128, 704, 2048], P(('expert', 'head')), may hold values from -0.125 to 0.125
- w_down: bfloat16 [128, 704, 2048], P(('expert', 'head')), may hold values from -0.15625 to 0.15625
- lengths: int32 [2], replicated, may hold values from 2048 to 8192, as said below
- expert_of_cell: int32 [8192, 2], P(('expert', 'head')), may hold values from 0 to 63, as said below
- slot_of_cell: int32 [8192, 2], P(('expert', 'head')), may hold values from 0 to 3, as said below
Outputs:
- updated_cells: bfloat16 [8192, 2, 2048], P(('expert', 'head'))
Inputs may be any that keep to these rules, and one draw needn't show every extreme that they name: `lengths`: one table in every draw has all 8192 cells. `expert_of_cell`: within the 128 cells of one device (aligned blocks in row-major order), no expert has more than 4 cells, and in every draw one expert has exactly 4 cells in every device's block. `slot_of_cell`: cells of one device with the same expert have distinct slots.
All inputs are finite; a program needn't handle non-finite values.
Results may differ from a plain program's by a relative error of at most 0.014.
Values may be sent and summed in bfloat16 or wider, within the bound.
A program may use at most 128 MiB of HBM per device.

v0:
```python
import math
import jax
import jax.numpy as jnp
from jax import lax
from jax.sharding import PartitionSpec as P

DH = 128


def expert_half(slot_rows, gate_half, up_half, down_half):
    contract_rows = (((1,), (1,)), ((), ()))
    gate_t = lax.dot_general(
        gate_half, slot_rows, contract_rows, preferred_element_type=jnp.float32
    )
    up_t = lax.dot_general(up_half, slot_rows, contract_rows, preferred_element_type=jnp.float32)
    hidden = (jax.nn.silu(gate_t) * up_t).astype(jnp.bfloat16)
    product = lax.dot_general(
        hidden, down_half, (((0,), (0,)), ((), ())), preferred_element_type=jnp.float32
    )
    return product.astype(jnp.bfloat16)


def shards(
    table_cells,
    w_query,
    w_key,
    w_value,
    w_out,
    norm_gain,
    w_gate,
    w_up,
    w_down,
    lengths,
    expert_of_cell,
    slot_of_cell,
):
    cell_count, tables, model_width = table_cells.shape
    head_width = w_query.shape[1]
    head_count = head_width // DH
    score_scale = 1.0 / math.sqrt(DH)
    joined = jnp.concatenate([w_query, w_key, w_value], axis=1)
    shard_rows = lax.all_gather(table_cells, "head", axis=0, tiled=True)
    rows_here = shard_rows.shape[0]
    mixed_rows = jnp.dot(
        shard_rows.reshape(rows_here * tables, model_width),
        joined,
        preferred_element_type=jnp.float32,
    )
    projected = mixed_rows.astype(jnp.bfloat16).reshape(rows_here, tables, 3 * head_width)
    row_cells = projected.shape[0]
    queries = projected[:, :, :head_width].reshape(row_cells, tables, head_count, DH)
    key_rows = projected[:, :, head_width : 2 * head_width]
    value_rows = projected[:, :, 2 * head_width :]
    offset = lax.axis_index("expert") * row_cells
    own_positions = offset + jnp.arange(row_cells, dtype=jnp.int32)
    start_state = (
        jnp.full((tables, head_count, row_cells), -1e30, jnp.float32),
        jnp.zeros((tables, head_count, row_cells), jnp.float32),
        jnp.zeros((tables, head_count, row_cells, DH), jnp.float32),
    )
    key_piece = lax.all_gather(key_rows, "expert", axis=0, tiled=True)
    value_piece = lax.all_gather(value_rows, "expert", axis=0, tiled=True)
    piece_len = key_piece.shape[0]
    block_len = math.gcd(piece_len, 512)
    block_count = piece_len // block_len
    key_blocks = key_piece.reshape(block_count, block_len, tables, head_count, DH)
    value_blocks = value_piece.reshape(block_count, block_len, tables, head_count, DH)
    block_starts = jnp.arange(block_count, dtype=jnp.int32) * block_len

    def step(carried, block_item):
        running_max, running_sum, accum = carried
        key_block, value_block, block_first = block_item
        scores = (
            jnp.einsum("qshd,kshd->shqk", queries, key_block, preferred_element_type=jnp.float32)
            * score_scale
        )
        key_valid = (block_first + jnp.arange(block_len, dtype=jnp.int32))[None, :] < lengths[
            :, None
        ]
        scores = jnp.where(key_valid[:, None, None, :], scores, -jnp.inf)
        new_max = jnp.maximum(running_max, jnp.max(scores, axis=-1))
        factor = jnp.exp(running_max - new_max)
        exp_scores = jnp.exp(scores - new_max[..., None])
        running_sum = running_sum * factor + jnp.sum(exp_scores, axis=-1)
        accum = accum * factor[..., None] + jnp.einsum(
            "shqk,kshd->shqd",
            exp_scores.astype(jnp.bfloat16),
            value_block,
            preferred_element_type=jnp.float32,
        )
        return ((new_max, running_sum, accum), None)

    finished, _ = lax.scan(step, start_state, (key_blocks, value_blocks, block_starts))
    running_max, running_sum, accum = finished
    normalized = accum / running_sum[..., None]
    live = own_positions[None, :] < lengths[:, None]
    normalized = jnp.where(live[:, None, :, None], normalized, 0.0)
    attended = (
        jnp.transpose(normalized, (2, 0, 1, 3))
        .reshape(row_cells, tables, head_width)
        .astype(jnp.bfloat16)
    )
    count_rows = cell_count * lax.axis_size("head")
    product = jnp.dot(
        attended.reshape(count_rows * tables, head_width), w_out, preferred_element_type=jnp.float32
    )
    summed = lax.psum_scatter(
        product.reshape(count_rows, tables, model_width).astype(jnp.bfloat16),
        "head",
        scatter_dimension=0,
        tiled=True,
    ).astype(jnp.float32)
    residual = table_cells.astype(jnp.float32) + summed
    mean_square = jnp.mean(residual * residual, axis=-1, keepdims=True)
    normed = (residual * lax.rsqrt(mean_square + 1e-06) * norm_gain.astype(jnp.float32)).astype(
        jnp.bfloat16
    )
    rows_dev = cell_count * tables
    normed_rows = normed.reshape(rows_dev, model_width)
    expert_count = lax.axis_size("expert") * lax.axis_size("head") // 2
    slot_cap = 2 * max(1, rows_dev // expert_count)
    target = expert_of_cell.reshape(rows_dev) * slot_cap + slot_of_cell.reshape(rows_dev)
    slot_table = (
        jnp.arange(expert_count * slot_cap, dtype=jnp.int32)[:, None] == target[None, :]
    ).astype(jnp.bfloat16)
    send_rows = jnp.dot(slot_table, normed_rows, preferred_element_type=jnp.float32).astype(
        jnp.bfloat16
    )
    gate_half = w_gate[0]
    up_half = w_up[0]
    down_half = w_down[0]
    doubled = jnp.repeat(send_rows.reshape(expert_count, slot_cap, model_width), 2, axis=0)
    received = lax.all_to_all(doubled, ("expert", "head"), split_axis=0, concat_axis=0, tiled=True)
    sources = received.shape[0]
    item_count = received.shape[1]
    flat_rows = received.reshape(sources * item_count, model_width)
    gathered = lax.all_to_all(
        expert_half(flat_rows, gate_half, up_half, down_half).reshape(
            sources, item_count, model_width
        ),
        ("expert", "head"),
        split_axis=0,
        concat_axis=0,
        tiled=True,
    )
    halves = gathered.reshape(expert_count, 2, slot_cap, model_width).astype(jnp.float32)
    combined = (
        (halves[:, 0] + halves[:, 1])
        .astype(jnp.bfloat16)
        .reshape(expert_count * slot_cap, model_width)
    )
    expert_out = lax.dot_general(
        slot_table, combined, (((0,), (0,)), ((), ())), preferred_element_type=jnp.float32
    )
    updated = (residual.reshape(rows_dev, model_width) + expert_out).astype(jnp.bfloat16)
    return updated.reshape(cell_count, tables, model_width)


def solution(mesh):
    placed = (
        P(("expert", "head"), None, None),
        P(None, "head"),
        P(None, "head"),
        P(None, "head"),
        P("head", None),
        P(),
        P(("expert", "head"), None, None),
        P(("expert", "head"), None, None),
        P(("expert", "head"), None, None),
        P(),
        P(("expert", "head"), None),
        P(("expert", "head"), None),
    )
    return jax.shard_map(
        shards,
        mesh=mesh,
        in_specs=placed,
        out_specs=P(("expert", "head"), None, None),
        check_vma=False,
    )
```

profile of v0, /device:TPU:1, one launch (start us, length us, event | category | flops | bytes accessed | tf_op | source)
XLA Modules:
  0.0 631.7 jit_solution(11269988385761301558)
XLA Ops:
  7.3 37.8 %all-gather.4.cloned.1.call-done = bf16[512,2,2048]{2,1,0:T(2,128)(2,1)} async-done(((bf16[64,2,2048]{2,1,0:T(2,128)(2,1)}), bf16[512,2,2048]{2,1,0:T(2,128)(2,1)}) %all-gather.4.cloned.1.call-update) | async-done | bytes 4194320 | tf_op jit(solution)/shard_map/all_gather | solution.py:42
  45.1 7.2 %reshape.135 = bf16[1024,2048]{1,0:T(8,128)(2,1)} reshape(bf16[512,2,2048]{2,1,0:T(2,128)(2,1)} %all-gather.4.cloned.1.call-done) | data formatting | bytes 8388608 | tf_op jit(solution)/shard_map/reshape | solution.py:45
  52.3 7.8 %fusion.33 = bf16[1024,768]{0,1:T(8,128)(2,1)} fusion(bf16[1024,2048]{1,0:T(8,128)(2,1)} %reshape.135, bf16[2048,256]{1,0:T(8,128)(2,1)} %param.17, bf16[2048,256]{1,0:T(8,128)(2,1)} %param.16, bf16[2048,256]{1,0:T(8,128)(2,1)} %param.15), kind=kOutput, calls=%fused_computation.46 | convolution fusion | flops 3231449088 | bytes 8912896 | tf_op jit(solution)/shard_map/dot_general | solution.py:44
  62.7 4.5 reshape.136
  74.5 66.3 %all-gather.6.cloned.1.call-done = bf16[8192,2,256]{2,1,0:T(2,128)(2,1)} async-done(((bf16[512,2,256]{2,1,0:T(2,128)(2,1)}), bf16[8192,2,256]{2,1,0:T(2,128)(2,1)}) %all-gather.6.cloned.1.call-update) | async-done | bytes 8388624 | tf_op jit(solution)/shard_map/all_gather | solution.py:61
  140.8 21.6 %reshape.149 = bf16[16,512,2,2,128]{4,3,2,1,0:T(2,128)(2,1)} reshape(bf16[8192,2,256]{2,1,0:T(2,128)(2,1)} %all-gather.6.cloned.1.call-done) | data formatting | bytes 16777216 | tf_op jit(solution)/shard_map/reshape | solution.py:66
  162.5 50.9 %all-gather.8.cloned.1.call-done = bf16[8192,2,256]{2,1,0:T(2,128)(2,1)} async-done(((bf16[512,2,256]{2,1,0:T(2,128)(2,1)}), bf16[8192,2,256]{2,1,0:T(2,128)(2,1)}) %all-gather.8.cloned.1.call-update) | async-done | bytes 8388624 | tf_op jit(solution)/shard_map/all_gather | solution.py:62
  213.3 21.6 %reshape.150 = bf16[16,512,2,2,128]{4,3,2,1,0:T(2,128)(2,1)} reshape(bf16[8192,2,256]{2,1,0:T(2,128)(2,1)} %all-gather.8.cloned.1.call-done) | data formatting | bytes 16777216 | tf_op jit(solution)/shard_map/reshape | solution.py:67
  234.9 227.6 %while.15 = (s32[]{:T(128)}, f32[2,2,512]{2,1,0:T(2,128)S(1)}, f32[2,2,512]{2,1,0:T(2,128)S(1)}, f32[2,2,512,128]{3,2,1,0:T(8,128)}, s32[16]{0:T(128)S(1)}, /*in...) while((s32[]{:T(128)}, f32[2,2,512]{2,1,0:T(2,128)S(1)}, ...), condition=%wide.region_3.4_spmd.clone, body=%wide.region_0.3_spmd.clone.sunk | while | flops 549203456 | bytes 35266736 | solution.py:93
  259.0 4.1 fusion.75
  301.7 4.1 fusion.75
  344.5 4.1 fusion.75
  358.7 4.1 fusion.75
  373.0 4.1 fusion.75
  387.2 4.1 fusion.75
  401.5 4.1 fusion.75
  466.5 4.5 convolution_convert_fusion
  471.9 34.2 %reduce-scatter.2.cloned.1.call-done = bf16[64,2,2048]{2,0,1:T(8,128)(2,1)} async-done(((bf16[512,2,2048]{2,0,1:T(8,128)(2,1)}), bf16[64,2,2048]{2,0,1:T(8,128)(2,1)}) %reduce-scatter.2.cloned.1.call-update) | async-done | bytes 524304 | tf_op jit(solution)/shard_map/reduce_scatter | solution.py:107
  518.5 40.4 %all_to_all.10 = bf16[128,4,2048]{2,1,0:T(4,128)(2,1)} all-to-all(bf16[128,4,2048]{2,1,0:T(4,128)(2,1)S(1)} %bitcast.83), channel_id=1, replica_groups=mesh['expert'=16,'head'=8] {'expert','head'}, dimensions={0} | all-to-all | bytes 4194304 | tf_op jit(solution)/shard_map/all_to_all | solution.py:133
  562.9 5.3 fusion.36
  568.1 7.6 %convolution_convert_fusion.1 = bf16[512,2048]{1,0:T(8,128)(2,1)} fusion(bf16[1,704,2048]{2,1,0:T(8,128)(2,1)S(1)} %copy-done, bf16[512,2048]{1,0:T(8,128)(2,1)} %reshape.144, bf16[1,704,2048]{2,1,0:T(8,128)(2,1)} %param.21, f32[704,512]{1,0:T(8,128)} %fusion.36), kind=kOutput, calls=%fused_computation.34 | convolution fusion | flops 2956001280 | bytes 11403264 | tf_op jit(solution)/shard_map/dot_general | solution.py:17
  575.8 4.1 reshape.145
  579.9 5.7 all-to-all-start.1
  591.5 24.4 %all-to-all-done.1 = bf16[128,4,2048]{2,1,0:T(4,128)(2,1)} async-done(((bf16[128,4,2048]{2,1,0:T(4,128)(2,1)}), bf16[128,4,2048]{2,1,0:T(4,128)(2,1)}, u32[]{:S(2)}, u32[]{:S(2)}) %all-to-all-start.1) | async-done | bytes 2097184 | tf_op jit(solution)/shard_map/all_to_all | solution.py:137
  (237 shorter events, 245.5 us)
Async XLA Ops:
  6.5 561.6 %copy-start = (bf16[1,704,2048]{2,1,0:T(8,128)(2,1)S(1)}, bf16[1,704,2048]{2,1,0:T(8,128)(2,1)}, u32[]{:S(2)}) copy-start(bf16[1,704,2048]{2,1,0:T(8,128)(2,1)} %param.22) | copy-start | bytes 8650756
  6.5 38.5 %all-gather.4.cloned.1.call-start = ((), (), s32[]{:S(2)}) async-start(), calls=%async_computation.3 | async-start | bytes 4718592 | tf_op jit(solution)/shard_map/all_gather | solution.py:42
  7.3 133.5 %all-gather.6.cloned.1.call-start = ((), (), s32[]{:S(2)}) async-start(), calls=%async_computation.4 | async-start | bytes 8912896 | tf_op jit(solution)/shard_map/all_gather | solution.py:61
  62.7 9.0 %copy-start.3 = (s32[2]{0:T(128)S(1)}, s32[2]{0:T(128)}, u32[]{:S(2)}) copy-start(s32[2]{0:T(128)} %param.23) | copy-start | bytes 28
  70.7 142.7 %all-gather.8.cloned.1.call-start = ((), (), s32[]{:S(2)}) async-start(), calls=%async_computation.5 | async-start | bytes 8912896 | tf_op jit(solution)/shard_map/all_gather | solution.py:62
  71.4 434.7 %reduce-scatter.2.cloned.1.call-start = ((), (), s32[]{:S(2)}) async-start(), calls=%async_computation.6 | async-start | bytes 4718592 | tf_op jit(solution)/shard_map/reduce_scatter | solution.py:107
  241.6 3.4 copy-start.1
  255.5 3.4 copy-start.1
  269.8 3.4 copy-start.1
  284.0 3.4 copy-start.1
  298.3 3.4 copy-start.1
  312.5 3.4 copy-start.1
  326.8 3.4 copy-start.1
  341.0 3.4 copy-start.1
  355.3 3.4 copy-start.1
  369.5 3.4 copy-start.1
  383.8 3.4 copy-start.1
  398.0 3.4 copy-start.1
  412.3 3.4 copy-start.1
  426.5 3.4 copy-start.1
  440.8 3.4 copy-start.1
  455.0 3.4 copy-start.1
  471.0 35.2 %copy-start.2 = (bf16[64,2,2048]{2,1,0:T(2,128)(2,1)S(1)}, bf16[64,2,2048]{2,1,0:T(2,128)(2,1)}, u32[]{:S(2)}) copy-start(bf16[64,2,2048]{2,1,0:T(2,128)(2,1)} %param.14) | copy-start | bytes 1572868
  579.9 36.0 %all-to-all-start.1 = ((bf16[128,4,2048]{2,1,0:T(4,128)(2,1)}), bf16[128,4,2048]{2,1,0:T(4,128)(2,1)}, u32[]{:S(2)}, u32[]{:S(2)}) async-start(bf16[128,4,2048]{2,1,0:T(4,128)(2,1)} %reshape.145), calls=%async_computation.2 | async-start | bytes 4194304 | tf_op jit(solution)/shard_map/all_to_all | solution.py:137
  (3 other events, 2.1 us)
Sparse Core Ops, SparseCore 0:
  9.1 35.9 all-gather.3
  70.8 69.9 all-gather.5
  143.0 70.3 all-gather.7
  471.1 34.9 reduce-scatter.1
where the time goes:
time: 635 us; the launch traced here: 632 us
  waiting for transfers between devices  215 us (34%)
  local copies, waits for them, and re-layouts  146 us (23%)
  matrix products  138 us (22%)
  other arithmetic  73.5 us (12%)
  blocking collectives  40.4 us (6%)
  between operations  13.2 us (2%)
    all_gather x1, waiting for transfers between devices, shards(): key_piece = lax.all_gather(key_rows, 'expert', axis=0, tiled=True)  66.3 us
    dot_general x16, matrix products, step(): jnp.einsum('shqk,kshd->shqd', exp_scores.astype(jnp.bfloat16), value_bloc...  65.2 us
    dynamic_slice x32, local copies, waits for them, and re-layouts, shards(): lax.scan(step, start_state, (key_blocks, value_blocks, block_starts))  52.7 us
    reduce_sum x16, other arithmetic, step(): running_sum = running_sum * factor + jnp.sum(exp_scores, axis=-1)  52.1 us
    all_gather x1, waiting for transfers between devices, shards(): value_piece = lax.all_gather(value_rows, 'expert', axis=0, tiled=True)  50.9 us
    dot_general x16, matrix products, step(): jnp.einsum('qshd,kshd->shqk', queries, key_block, preferred_element_type=...  42.8 us
    all_to_all x1, blocking collectives, shards(): lax.all_to_all(doubled, ('expert', 'head'), split_axis=0, concat_axis=0,...  40.4 us
    all_gather x1, waiting for transfers between devices, shards(): shard_rows = lax.all_gather(table_cells, 'head', axis=0, tiled=True)  37.8 us
  transfers between devices with their start and end apart: 5, of which 5 were waited for; matrix products, arithmetic and copies ran while one was open for 5% of the time, Pallas kernels for 0%

commit v1 on v0

--- a/solution.py
+++ b/solution.py
@@ -58,7 +58,14 @@
         jnp.zeros((tables, head_count, row_cells), jnp.float32),
         jnp.zeros((tables, head_count, row_cells, DH), jnp.float32),
     )
-    key_piece = lax.all_gather(key_rows, "expert", axis=0, tiled=True)
+    ring = [key_rows]
+    for hop in range(15):
+        ring.append(lax.ppermute(ring[-1], "expert", [(dev, (dev + 1) % 16) for dev in range(16)]))
+    key_piece = jnp.roll(
+        jnp.concatenate(ring[::-1], axis=0),
+        (lax.axis_index("expert") + 1) * ring[0].shape[0],
+        axis=0,
+    )
     value_piece = lax.all_gather(value_rows, "expert", axis=0, tiled=True)
     piece_len = key_piece.shape[0]
     block_len = math.gcd(piece_len, 512)

time: 635 us -> 838 us (1.32)
  waiting for transfers between devices: 215 us -> 359 us
  local copies, waits for them, and re-layouts: 146 us -> 179 us
  matrix products: 138 us -> 156 us
    ppermute x0 -> x15, waiting for transfers between devices: none -> 214 us  [shards(): lax.ppermute(ring[-1], 'expert', [(dev, (dev + 1) % 16) for dev in range(...]
    all_gather x1 -> x0, waiting for transfers between devices: 66.3 us -> none  [shards(): key_piece = lax.all_gather(key_rows, 'expert', axis=0, tiled=True)]
    unnamed x13 -> x48, local copies, waits for them, and re-layouts: 2 us -> 29.3 us
    dot_general x16, matrix products: 65.2 us -> 84.2 us  [step(): jnp.einsum('shqk,kshd->shqd', exp_scores.astype(jnp.bfloat16), value_bloc...]
  transfers between devices with their start and end apart: 5 -> 19, of which waited for: 5 -> 19; matrix products, arithmetic and copies ran while one was open for 5% -> 5% of each run, Pallas kernels for 0% -> 0%
where the time goes in v1:
time: 838 us; the launch traced here: 827 us
  waiting for transfers between devices  359 us (43%)
  local copies, waits for them, and re-layouts  179 us (21%)
  matrix products  156 us (19%)
  other arithmetic  71 us (8%)
  blocking collectives  40.4 us (5%)
  between operations  13.8 us (2%)
    ppermute x15, waiting for transfers between devices, shards(): lax.ppermute(ring[-1], 'expert', [(dev, (dev + 1) % 16) for dev in range(...  214 us
    dot_general x16, matrix products, step(): jnp.einsum('shqk,kshd->shqd', exp_scores.astype(jnp.bfloat16), value_bloc...  84.2 us
    dynamic_slice x32, local copies, waits for them, and re-layouts, shards(): lax.scan(step, start_state, (key_blocks, value_blocks, block_starts))  52.7 us
    reduce_sum x16, other arithmetic, step(): running_sum = running_sum * factor + jnp.sum(exp_scores, axis=-1)  49.7 us
    all_gather x1, waiting for transfers between devices, shards(): value_piece = lax.all_gather(value_rows, 'expert', axis=0, tiled=True)  47.3 us
    dot_general x16, matrix products, step(): jnp.einsum('qshd,kshd->shqk', queries, key_block, preferred_element_type=...  42.7 us
    all_to_all x1, blocking collectives, shards(): lax.all_to_all(doubled, ('expert', 'head'), split_axis=0, concat_axis=0,...  40.4 us
    all_gather x1, waiting for transfers between devices, shards(): shard_rows = lax.all_gather(table_cells, 'head', axis=0, tiled=True)  37.8 us
  transfers between devices with their start and end apart: 19, of which 19 were waited for; matrix products, arithmetic and copies ran while one was open for 5% of the time, Pallas kernels for 0%

profile of v1, /device:TPU:1, one launch (start us, length us, event | category | flops | bytes accessed | tf_op | source)
XLA Modules:
  0.0 827.1 jit_solution(1955717727188153227)
XLA Ops:
  7.3 37.8 %all-gather.3.cloned.1.call-done = bf16[512,2,2048]{2,1,0:T(2,128)(2,1)} async-done(((bf16[64,2,2048]{2,1,0:T(2,128)(2,1)}), bf16[512,2,2048]{2,1,0:T(2,128)(2,1)}) %all-gather.3.cloned.1.call-update) | async-done | bytes 4194320 | tf_op jit(solution)/shard_map/all_gather | solution.py:42
  70.0 15.4 %collective-permute-done = bf16[512,2,256]{2,1,0:T(2,128)(2,1)S(1)} collective-permute-done((bf16[512,2,256]{2,1,0:T(2,128)(2,1)S(1)}, bf16[512,2,256]{2,1,0:T(2,128)(2,1)S(1)}, u32[]{:S(2)}, u32[]{:S(2)}) %collective-permute-start) | collective-permute-done | bytes 524320 | tf_op jit(solution)/shard_map/ppermute | solution.py:63
  85.3 15.7 %collective-permute-done.1 = bf16[512,2,256]{2,1,0:T(2,128)(2,1)S(1)} collective-permute-done((bf16[512,2,256]{2,1,0:T(2,128)(2,1)S(1)}, bf16[512,2,256]{2,1,0:T(2,128)(2,1)S(1)}, u32[]{:S(2)}, u32[]{:S(2)}) %collective-permute-start.1) | collective-permute-done | bytes 524320 | tf_op jit(solution)/shard_map/ppermute | solution.py:63
  101.0 14.7 %collective-permute-done.2 = bf16[512,2,256]{2,1,0:T(2,128)(2,1)S(1)} collective-permute-done((bf16[512,2,256]{2,1,0:T(2,128)(2,1)S(1)}, bf16[512,2,256]{2,1,0:T(2,128)(2,1)S(1)}, u32[]{:S(2)}, u32[]{:S(2)}) %collective-permute-start.2) | collective-permute-done | bytes 524320 | tf_op jit(solution)/shard_map/ppermute | solution.py:63
  115.8 13.8 %collective-permute-done.3 = bf16[512,2,256]{2,1,0:T(2,128)(2,1)S(1)} collective-permute-done((bf16[512,2,256]{2,1,0:T(2,128)(2,1)S(1)}, bf16[512,2,256]{2,1,0:T(2,128)(2,1)S(1)}, u32[]{:S(2)}, u32[]{:S(2)}) %collective-permute-start.3) | collective-permute-done | bytes 524320 | tf_op jit(solution)/shard_map/ppermute | solution.py:63
  129.6 12.9 %collective-permute-done.4 = bf16[512,2,256]{2,1,0:T(2,128)(2,1)S(1)} collective-permute-done((bf16[512,2,256]{2,1,0:T(2,128)(2,1)S(1)}, bf16[512,2,256]{2,1,0:T(2,128)(2,1)S(1)}, u32[]{:S(2)}, u32[]{:S(2)}) %collective-permute-start.4) | collective-permute-done | bytes 524320 | tf_op jit(solution)/shard_map/ppermute | solution.py:63
  142.5 12.0 %collective-permute-done.5 = bf16[512,2,256]{2,1,0:T(2,128)(2,1)S(1)} collective-permute-done((bf16[512,2,256]{2,1,0:T(2,128)(2,1)S(1)}, bf16[512,2,256]{2,1,0:T(2,128)(2,1)S(1)}, u32[]{:S(2)}, u32[]{:S(2)}) %collective-permute-start.5) | collective-permute-done | bytes 524320 | tf_op jit(solution)/shard_map/ppermute | solution.py:63
  154.4 11.3 %collective-permute-done.6 = bf16[512,2,256]{2,1,0:T(2,128)(2,1)S(1)} collective-permute-done((bf16[512,2,256]{2,1,0:T(2,128)(2,1)S(1)}, bf16[512,2,256]{2,1,0:T(2,128)(2,1)S(1)}, u32[]{:S(2)}, u32[]{:S(2)}) %collective-permute-start.6) | collective-permute-done | bytes 524320 | tf_op jit(solution)/shard_map/ppermute | solution.py:63
  165.8 11.8 %collective-permute-done.7 = bf16[512,2,256]{2,1,0:T(2,128)(2,1)S(1)} collective-permute-done((bf16[512,2,256]{2,1,0:T(2,128)(2,1)S(1)}, bf16[512,2,256]{2,1,0:T(2,128)(2,1)S(1)}, u32[]{:S(2)}, u32[]{:S(2)}) %collective-permute-start.7) | collective-permute-done | bytes 524320 | tf_op jit(solution)/shard_map/ppermute | solution.py:63
  177.6 12.8 %collective-permute-done.8 = bf16[512,2,256]{2,1,0:T(2,128)(2,1)S(1)} collective-permute-done((bf16[512,2,256]{2,1,0:T(2,128)(2,1)S(1)}, bf16[512,2,256]{2,1,0:T(2,128)(2,1)S(1)}, u32[]{:S(2)}, u32[]{:S(2)}) %collective-permute-start.8) | collective-permute-done | bytes 524320 | tf_op jit(solution)/shard_map/ppermute | solution.py:63
  190.4 13.9 %collective-permute-done.9 = bf16[512,2,256]{2,1,0:T(2,128)(2,1)S(1)} collective-permute-done((bf16[512,2,256]{2,1,0:T(2,128)(2,1)S(1)}, bf16[512,2,256]{2,1,0:T(2,128)(2,1)S(1)}, u32[]{:S(2)}, u32[]{:S(2)}) %collective-permute-start.9) | collective-permute-done | bytes 524320 | tf_op jit(solution)/shard_map/ppermute | solution.py:63
  204.3 15.0 %collective-permute-done.10 = bf16[512,2,256]{2,1,0:T(2,128)(2,1)S(1)} collective-permute-done((bf16[512,2,256]{2,1,0:T(2,128)(2,1)S(1)}, bf16[512,2,256]{2,1,0:T(2,128)(2,1)S(1)}, u32[]{:S(2)}, u32[]{:S(2)}) %collective-permute-start.10) | collective-permute-done | bytes 524320 | tf_op jit(solution)/shard_map/ppermute | solution.py:63
  219.3 16.1 %collective-permute-done.11 = bf16[512,2,256]{2,1,0:T(2,128)(2,1)S(1)} collective-permute-done((bf16[512,2,256]{2,1,0:T(2,128)(2,1)S(1)}, bf16[512,2,256]{2,1,0:T(2,128)(2,1)S(1)}, u32[]{:S(2)}, u32[]{:S(2)}) %collective-permute-start.11) | collective-permute-done | bytes 524320 | tf_op jit(solution)/shard_map/ppermute | solution.py:63
  235.4 17.0 %collective-permute-done.12 = bf16[512,2,256]{2,1,0:T(2,128)(2,1)S(1)} collective-permute-done((bf16[512,2,256]{2,1,0:T(2,128)(2,1)S(1)}, bf16[512,2,256]{2,1,0:T(2,128)(2,1)S(1)}, u32[]{:S(2)}, u32[]{:S(2)}) %collective-permute-start.12) | collective-permute-done | bytes 524320 | tf_op jit(solution)/shard_map/ppermute | solution.py:63
  252.4 16.1 %collective-permute-done.13 = bf16[512,2,256]{2,1,0:T(2,128)(2,1)S(1)} collective-permute-done((bf16[512,2,256]{2,1,0:T(2,128)(2,1)S(1)}, bf16[512,2,256]{2,1,0:T(2,128)(2,1)S(1)}, u32[]{:S(2)}, u32[]{:S(2)}) %collective-permute-start.13) | collective-permute-done | bytes 524320 | tf_op jit(solution)/shard_map/ppermute | solution.py:63
  268.8 15.4 %collective-permute-done.14 = bf16[512,2,256]{2,1,0:T(2,128)(2,1)S(1)} collective-permute-done((bf16[512,2,256]{2,1,0:T(2,128)(2,1)S(1)}, bf16[512,2,256]{2,1,0:T(2,128)(2,1)S(1)}, u32[]{:S(2)}, u32[]{:S(2)}) %collective-permute-start.14) | collective-permute-done | bytes 524320 | tf_op jit(solution)/shard_map/ppermute | solution.py:63
  295.4 10.2 %constant_dynamic-update-slice_fusion.3 = bf16[16384,2,256]{2,1,0:T(2,128)(2,1)S(1)} fusion(bf16[16384,2,256]{2,1,0:T(2,128)(2,1)S(1)} %constant_dynamic-update-slice_fusion.4, bf16[512,2,256]{2,1,0:T(2,128)(2,1)S(1)} %collective-permute-done.2), kind=kLoop, calls=%fused_computation.61 | loop fusion | bytes 1048576
  322.3 21.7 %reshape.149 = bf16[16,512,2,2,128]{4,3,2,1,0:T(2,128)(2,1)} reshape(bf16[8192,2,256]{2,1,0:T(2,128)(2,1)} %constant_dynamic-slice_fusion.2) | data formatting | bytes 16777216 | tf_op jit(solution)/shard_map/reshape | solution.py:73
  346.8 47.3 %all-gather.5.cloned.1.call-done = bf16[8192,2,256]{2,1,0:T(2,128)(2,1)} async-done(((bf16[512,2,256]{2,1,0:T(2,128)(2,1)}), bf16[8192,2,256]{2,1,0:T(2,128)(2,1)}) %all-gather.5.cloned.1.call-update) | async-done | bytes 8388624 | tf_op jit(solution)/shard_map/all_gather | solution.py:69
  394.0 21.6 %reshape.150 = bf16[16,512,2,2,128]{4,3,2,1,0:T(2,128)(2,1)} reshape(bf16[8192,2,256]{2,1,0:T(2,128)(2,1)} %all-gather.5.cloned.1.call-done) | data formatting | bytes 16777216 | tf_op jit(solution)/shard_map/reshape | solution.py:74
  415.6 241.8 %while.15 = (s32[]{:T(128)}, f32[2,2,512]{2,1,0:T(2,128)S(1)}, f32[2,2,512]{2,1,0:T(2,128)S(1)}, f32[2,2,512,128]{3,2,1,0:T(8,128)}, s32[16]{0:T(128)S(1)}, /*in...) while((s32[]{:T(128)}, f32[2,2,512]{2,1,0:T(2,128)S(1)}, ...), condition=%wide.region_3.4_spmd.clone, body=%wide.region_0.3_spmd.clone.sunk | while | flops 549203456 | bytes 18489492 | solution.py:100
  666.2 34.8 %reduce-scatter.2.cloned.1.call-done = bf16[64,2,2048]{2,0,1:T(8,128)(2,1)} async-done(((bf16[512,2,2048]{2,0,1:T(8,128)(2,1)}), bf16[64,2,2048]{2,0,1:T(8,128)(2,1)}) %reduce-scatter.2.cloned.1.call-update) | async-done | bytes 524304 | tf_op jit(solution)/shard_map/reduce_scatter | solution.py:114
  713.6 40.4 %all_to_all.10 = bf16[128,4,2048]{2,1,0:T(4,128)(2,1)} all-to-all(bf16[128,4,2048]{2,1,0:T(4,128)(2,1)S(1)} %bitcast.83), channel_id=1, replica_groups=mesh['expert'=16,'head'=8] {'expert','head'}, dimensions={0} | all-to-all | bytes 4194304 | tf_op jit(solution)/shard_map/all_to_all | solution.py:140
  786.6 24.3 %all-to-all-done.1 = bf16[128,4,2048]{2,1,0:T(4,128)(2,1)} async-done(((bf16[128,4,2048]{2,1,0:T(4,128)(2,1)}), bf16[128,4,2048]{2,1,0:T(4,128)(2,1)}, u32[]{:S(2)}, u32[]{:S(2)}) %all-to-all-start.1) | async-done | bytes 2097184 | tf_op jit(solution)/shard_map/all_to_all | solution.py:144
  (269 shorter events, 361.1 us)
Async XLA Ops:
  6.5 756.7 %copy-start = (bf16[1,704,2048]{2,1,0:T(8,128)(2,1)S(1)}, bf16[1,704,2048]{2,1,0:T(8,128)(2,1)}, u32[]{:S(2)}) copy-start(bf16[1,704,2048]{2,1,0:T(8,128)(2,1)} %param.22) | copy-start | bytes 8650756
  6.5 38.5 %all-gather.3.cloned.1.call-start = ((), (), s32[]{:S(2)}) async-start(), calls=%async_computation.3 | async-start | bytes 4718592 | tf_op jit(solution)/shard_map/all_gather | solution.py:42
  7.3 386.8 %all-gather.5.cloned.1.call-start = ((), (), s32[]{:S(2)}) async-start(), calls=%async_computation.4 | async-start | bytes 8912896 | tf_op jit(solution)/shard_map/all_gather | solution.py:69
  67.2 223.0 %copy-start.1 = (bf16[512,2,768]{2,1,0:T(2,128)(2,1)S(1)}, bf16[512,2,768]{2,1,0:T(2,128)(2,1)}, u32[]{:S(2)}) copy-start(bf16[512,2,768]{2,1,0:T(2,128)(2,1)} %reshape.136) | copy-start | bytes 4718596
  68.7 16.7 %collective-permute-start = (bf16[512,2,256]{2,1,0:T(2,128)(2,1)S(1)}, bf16[512,2,256]{2,1,0:T(2,128)(2,1)S(1)}, u32[]{:S(2)}, u32[]{:S(2)}) collective-permute-start(bf16[512,2,256]{2,1,0:T(2,128)(2,1)S(1)} %slice.20), channel_id=1, source_target_pairs={{0,8},{8,16},{16,24},{24,32},{32,40},{40,48},{48,56},{56,64},{64,7... | collective-permute-start | bytes 1572872 | tf_op jit(solution)/shard_map/ppermute | solution.py:63
  85.3 15.7 %collective-permute-start.1 = (bf16[512,2,256]{2,1,0:T(2,128)(2,1)S(1)}, bf16[512,2,256]{2,1,0:T(2,128)(2,1)S(1)}, u32[]{:S(2)}, u32[]{:S(2)}) collective-permute-start(bf16[512,2,256]{2,1,0:T(2,128)(2,1)S(1)} %collective-permute-done), channel_id=1, source_target_pairs={{0,8},{8,16},{16,24},{24,32},{32,40},{40,48},{48,56},{56,64},{64,7... | collective-permute-start | bytes 1572872 | tf_op jit(solution)/shard_map/ppermute | solution.py:63
  101.0 14.7 %collective-permute-start.2 = (bf16[512,2,256]{2,1,0:T(2,128)(2,1)S(1)}, bf16[512,2,256]{2,1,0:T(2,128)(2,1)S(1)}, u32[]{:S(2)}, u32[]{:S(2)}) collective-permute-start(bf16[512,2,256]{2,1,0:T(2,128)(2,1)S(1)} %collective-permute-done.1), channel_id=1, source_target_pairs={{0,8},{8,16},{16,24},{24,32},{32,40},{40,48},{48,56},{56,64},{64,7... | collective-permute-start | bytes 1572872 | tf_op jit(solution)/shard_map/ppermute | solution.py:63
  115.7 13.8 %collective-permute-start.3 = (bf16[512,2,256]{2,1,0:T(2,128)(2,1)S(1)}, bf16[512,2,256]{2,1,0:T(2,128)(2,1)S(1)}, u32[]{:S(2)}, u32[]{:S(2)}) collective-permute-start(bf16[512,2,256]{2,1,0:T(2,128)(2,1)S(1)} %collective-permute-done.2), channel_id=1, source_target_pairs={{0,8},{8,16},{16,24},{24,32},{32,40},{40,48},{48,56},{56,64},{64,7... | collective-permute-start | bytes 1572872 | tf_op jit(solution)/shard_map/ppermute | solution.py:63
  129.6 12.9 %collective-permute-start.4 = (bf16[512,2,256]{2,1,0:T(2,128)(2,1)S(1)}, bf16[512,2,256]{2,1,0:T(2,128)(2,1)S(1)}, u32[]{:S(2)}, u32[]{:S(2)}) collective-permute-start(bf16[512,2,256]{2,1,0:T(2,128)(2,1)S(1)} %collective-permute-done.3), channel_id=1, source_target_pairs={{0,8},{8,16},{16,24},{24,32},{32,40},{40,48},{48,56},{56,64},{64,7... | collective-permute-start | bytes 1572872 | tf_op jit(solution)/shard_map/ppermute | solution.py:63
  142.5 12.0 %collective-permute-start.5 = (bf16[512,2,256]{2,1,0:T(2,128)(2,1)S(1)}, bf16[512,2,256]{2,1,0:T(2,128)(2,1)S(1)}, u32[]{:S(2)}, u32[]{:S(2)}) collective-permute-start(bf16[512,2,256]{2,1,0:T(2,128)(2,1)S(1)} %collective-permute-done.4), channel_id=1, source_target_pairs={{0,8},{8,16},{16,24},{24,32},{32,40},{40,48},{48,56},{56,64},{64,7... | collective-permute-start | bytes 1572872 | tf_op jit(solution)/shard_map/ppermute | solution.py:63
  154.4 11.4 %collective-permute-start.6 = (bf16[512,2,256]{2,1,0:T(2,128)(2,1)S(1)}, bf16[512,2,256]{2,1,0:T(2,128)(2,1)S(1)}, u32[]{:S(2)}, u32[]{:S(2)}) collective-permute-start(bf16[512,2,256]{2,1,0:T(2,128)(2,1)S(1)} %collective-permute-done.5), channel_id=1, source_target_pairs={{0,8},{8,16},{16,24},{24,32},{32,40},{40,48},{48,56},{56,64},{64,7... | collective-permute-start | bytes 1572872 | tf_op jit(solution)/shard_map/ppermute | solution.py:63
  165.8 11.8 %collective-permute-start.7 = (bf16[512,2,256]{2,1,0:T(2,128)(2,1)S(1)}, bf16[512,2,256]{2,1,0:T(2,128)(2,1)S(1)}, u32[]{:S(2)}, u32[]{:S(2)}) collective-permute-start(bf16[512,2,256]{2,1,0:T(2,128)(2,1)S(1)} %collective-permute-done.6), channel_id=1, source_target_pairs={{0,8},{8,16},{16,24},{24,32},{32,40},{40,48},{48,56},{56,64},{64,7... | collective-permute-start | bytes 1572872 | tf_op jit(solution)/shard_map/ppermute | solution.py:63
  177.6 12.8 %collective-permute-start.8 = (bf16[512,2,256]{2,1,0:T(2,128)(2,1)S(1)}, bf16[512,2,256]{2,1,0:T(2,128)(2,1)S(1)}, u32[]{:S(2)}, u32[]{:S(2)}) collective-permute-start(bf16[512,2,256]{2,1,0:T(2,128)(2,1)S(1)} %collective-permute-done.7), channel_id=1, source_target_pairs={{0,8},{8,16},{16,24},{24,32},{32,40},{40,48},{48,56},{56,64},{64,7... | collective-permute-start | bytes 1572872 | tf_op jit(solution)/shard_map/ppermute | solution.py:63
  190.4 13.9 %collective-permute-start.9 = (bf16[512,2,256]{2,1,0:T(2,128)(2,1)S(1)}, bf16[512,2,256]{2,1,0:T(2,128)(2,1)S(1)}, u32[]{:S(2)}, u32[]{:S(2)}) collective-permute-start(bf16[512,2,256]{2,1,0:T(2,128)(2,1)S(1)} %collective-permute-done.8), channel_id=1, source_target_pairs={{0,8},{8,16},{16,24},{24,32},{32,40},{40,48},{48,56},{56,64},{64,7... | collective-permute-start | bytes 1572872 | tf_op jit(solution)/shard_map/ppermute | solution.py:63
  204.3 15.0 %collective-permute-start.10 = (bf16[512,2,256]{2,1,0:T(2,128)(2,1)S(1)}, bf16[512,2,256]{2,1,0:T(2,128)(2,1)S(1)}, u32[]{:S(2)}, u32[]{:S(2)}) collective-permute-start(bf16[512,2,256]{2,1,0:T(2,128)(2,1)S(1)} %collective-permute-done.9), channel_id=1, source_target_pairs={{0,8},{8,16},{16,24},{24,32},{32,40},{40,48},{48,56},{56,64},{64,7... | collective-permute-start | bytes 1572872 | tf_op jit(solution)/shard_map/ppermute | solution.py:63
  219.3 16.1 %collective-permute-start.11 = (bf16[512,2,256]{2,1,0:T(2,128)(2,1)S(1)}, bf16[512,2,256]{2,1,0:T(2,128)(2,1)S(1)}, u32[]{:S(2)}, u32[]{:S(2)}) collective-permute-start(bf16[512,2,256]{2,1,0:T(2,128)(2,1)S(1)} %collective-permute-done.10), channel_id=1, source_target_pairs={{0,8},{8,16},{16,24},{24,32},{32,40},{40,48},{48,56},{56,64},{64,7... | collective-permute-start | bytes 1572872 | tf_op jit(solution)/shard_map/ppermute | solution.py:63
  235.4 17.0 %collective-permute-start.12 = (bf16[512,2,256]{2,1,0:T(2,128)(2,1)S(1)}, bf16[512,2,256]{2,1,0:T(2,128)(2,1)S(1)}, u32[]{:S(2)}, u32[]{:S(2)}) collective-permute-start(bf16[512,2,256]{2,1,0:T(2,128)(2,1)S(1)} %collective-permute-done.11), channel_id=1, source_target_pairs={{0,8},{8,16},{16,24},{24,32},{32,40},{40,48},{48,56},{56,64},{64,7... | collective-permute-start | bytes 1572872 | tf_op jit(solution)/shard_map/ppermute | solution.py:63
  252.4 16.1 %collective-permute-start.13 = (bf16[512,2,256]{2,1,0:T(2,128)(2,1)S(1)}, bf16[512,2,256]{2,1,0:T(2,128)(2,1)S(1)}, u32[]{:S(2)}, u32[]{:S(2)}) collective-permute-start(bf16[512,2,256]{2,1,0:T(2,128)(2,1)S(1)} %collective-permute-done.12), channel_id=1, source_target_pairs={{0,8},{8,16},{16,24},{24,32},{32,40},{40,48},{48,56},{56,64},{64,7... | collective-permute-start | bytes 1572872 | tf_op jit(solution)/shard_map/ppermute | solution.py:63
  268.5 15.7 %collective-permute-start.14 = (bf16[512,2,256]{2,1,0:T(2,128)(2,1)S(1)}, bf16[512,2,256]{2,1,0:T(2,128)(2,1)S(1)}, u32[]{:S(2)}, u32[]{:S(2)}) collective-permute-start(bf16[512,2,256]{2,1,0:T(2,128)(2,1)S(1)} %collective-permute-done.13), channel_id=1, source_target_pairs={{0,8},{8,16},{16,24},{24,32},{32,40},{40,48},{48,56},{56,64},{64,7... | collective-permute-start | bytes 1572872 | tf_op jit(solution)/shard_map/ppermute | solution.py:63
  291.8 22.5 %copy-start.4 = (s32[2]{0:T(128)S(1)}, s32[2]{0:T(128)}, u32[]{:S(2)}) copy-start(s32[2]{0:T(128)} %param.23) | copy-start | bytes 28
  314.1 386.9 %reduce-scatter.2.cloned.1.call-start = ((), (), s32[]{:S(2)}) async-start(), calls=%async_computation.5 | async-start | bytes 4718592 | tf_op jit(solution)/shard_map/reduce_scatter | solution.py:114
  657.4 8.5 %copy-start.7 = (s32[64,2]{0,1:T(2,128)S(1)}, s32[64,2]{0,1:T(2,128)}, u32[]{:S(2)}) copy-start(s32[64,2]{0,1:T(2,128)} %param.24) | copy-start | bytes 1540
  657.4 43.6 %copy-start.3 = (bf16[64,2,2048]{2,1,0:T(2,128)(2,1)S(1)}, bf16[64,2,2048]{2,1,0:T(2,128)(2,1)}, u32[]{:S(2)}) copy-start(bf16[64,2,2048]{2,1,0:T(2,128)(2,1)} %param.14) | copy-start | bytes 1572868
  775.0 36.0 %all-to-all-start.1 = ((bf16[128,4,2048]{2,1,0:T(4,128)(2,1)}), bf16[128,4,2048]{2,1,0:T(4,128)(2,1)}, u32[]{:S(2)}, u32[]{:S(2)}) async-start(bf16[128,4,2048]{2,1,0:T(4,128)(2,1)} %reshape.145), calls=%async_computation.2 | async-start | bytes 4194304 | tf_op jit(solution)/shard_map/all_to_all | solution.py:144
  (3 other events, 22.8 us)
Sparse Core Ops, SparseCore 0:
  9.1 35.9 all-gather.2
  314.2 79.7 all-gather.4
  666.1 34.9 reduce-scatter.1
